TPU v7x, 256 devices: a whole 4x4x8 slice. The times are simulated.
256 devices in a mesh: req: 16 (over z, core), mp: 16 (over x, y).
Axes of the slice: x: 4, y: 4, z: 8, core: 2. Of those that a mesh axis runs over, the one named last changes fastest.
Arguments:
- tokens_in: bfloat16 [2048, 2048], P('req', 'mp'), may hold values from -6 to 6
- req_lengths: int32 [16, 4], replicated, may hold values from 1 to 64, 128 in all within a row
- req_groups: int32 [16, 4], replicated, may hold values from 0 to 1
- prefix_cache: bfloat16 [2, 4096, 2, 2048], P(None, 'req', None, 'mp'), may hold values from -170 to 170, as said below
- attn_gain: bfloat16 [2048], replicated, may hold values from 0.25 to 1.75
- mlp_gain: bfloat16 [2048], replicated, may hold values from 0.25 to 1.75
- w_qkv: bfloat16 [2048, 3, 2048], P(None, None, 'mp'), may hold values from -0.25 to 0.25
- w_out: bfloat16 [2048, 2048], P('mp'), may hold values from -0.1875 to 0.1875
- w_gate_up: bfloat16 [2048, 2, 5632], P(None, None, 'mp'), may hold values from -0.125 to 0.125
- w_down: bfloat16 [5632, 2048], P('mp'), may hold values from -0.109375 to 0.109375
Outputs:
- layer_out: bfloat16 [2048, 2048], P('req', 'mp')
Inputs may be any that keep to these rules, and one draw needn't show every extreme that they name: `req_lengths`: in each row the 4 lengths sum to 128, and the largest is 64. `prefix_cache`: keys are cached after rotation.
All inputs are finite; a program needn't handle non-finite values.
Results may differ from a plain program's by a relative error of at most 0.02.
The roundings to bfloat16 on the way count: a program that leaves them out, or rounds other values in their place, can miss the bound.
Values may be sent and summed in bfloat16 or wider, within the bound.
A program may use at most 64 MiB of HBM per device.

v0:
```python
import jax
import jax.numpy as jnp
from jax import lax
from jax.sharding import PartitionSpec as P

HEAD_DIM = 64
ROT = 16
PREFIX = 4096
GROUPS = 2
NEG = -1e30
EPS = 1e-05


def layer_norm(rows_in, gain_vec):
    values_f = rows_in.astype(jnp.float32)
    row_mean = jnp.mean(values_f, axis=-1, keepdims=True)
    centred = values_f - row_mean
    variance = jnp.mean(centred * centred, axis=-1, keepdims=True)
    return (centred * lax.rsqrt(variance + EPS) * gain_vec.astype(jnp.float32)).astype(jnp.bfloat16)


def rotary(vectors, positions):
    half_rot = ROT // 2
    frequency = 10000.0 ** (-(jnp.arange(half_rot, dtype=jnp.float32) * 2.0 / ROT))
    angles = positions[:, None] * frequency[None, :]
    cosine = jnp.cos(angles)[:, None, :]
    sine_part = jnp.sin(angles)[:, None, :]
    lower_half = vectors[..., :half_rot]
    upper_half = vectors[..., half_rot:ROT]
    return jnp.concatenate(
        [
            lower_half * cosine - upper_half * sine_part,
            upper_half * cosine + lower_half * sine_part,
            vectors[..., ROT:],
        ],
        axis=-1,
    )


def token_meta(length_row, group_row, row_count):
    starts = jnp.cumsum(length_row) - length_row
    places = jnp.arange(row_count, dtype=jnp.int32)
    request = jnp.sum((places[:, None] >= starts[None, :]).astype(jnp.int32), axis=1) - 1
    onehot = (request[:, None] == jnp.arange(length_row.shape[0], dtype=jnp.int32)[None, :]).astype(
        jnp.int32
    )
    offset = places - jnp.sum(onehot * starts[None, :], axis=1)
    groups_of = jnp.sum(onehot * group_row[None, :], axis=1)
    return (request, offset, groups_of)


def combine_states(state_a, state_b):
    mixed_a, top_a, sum_a = state_a
    mixed_b, top_b, sum_b = state_b
    top_new = jnp.maximum(top_a, top_b)
    scale_a = jnp.exp(top_a - top_new)
    scale_b = jnp.exp(top_b - top_new)
    return (
        mixed_a * scale_a[..., None] + mixed_b * scale_b[..., None],
        top_new,
        sum_a * scale_a + sum_b * scale_b,
    )


def rounded_block(query, member, part):
    group_count = part.shape[0]
    block = part.shape[1]
    row_count = query.shape[0]
    heads = query.shape[1]
    key_part = part[:, :, 0].reshape(group_count, block, heads, HEAD_DIM)
    value_part = part[:, :, 1].reshape(group_count * block, heads, HEAD_DIM)
    scores = jnp.einsum(
        "thd,gnhd->htgn", query, key_part, preferred_element_type=jnp.float32
    ) * HEAD_DIM ** (-0.5)
    scores = jnp.where(member[None, :, :, None], scores, NEG).reshape(
        heads, row_count, group_count * block
    )
    top_score = jnp.max(scores, axis=2)
    weights = jnp.exp(scores - top_score[:, :, None])
    weight_sum = jnp.sum(weights, axis=2)
    mixed_out = jnp.einsum(
        "hts,she->the", weights.astype(jnp.bfloat16), value_part, preferred_element_type=jnp.float32
    )
    normed_part = (mixed_out / weight_sum.T[..., None]).astype(jnp.bfloat16)
    return (normed_part, top_score.T, weight_sum.T)


def own_attention(query, keys, values, request, offset):
    scores = jnp.einsum(
        "thd,shd->hts", query, keys, preferred_element_type=jnp.float32
    ) * HEAD_DIM ** (-0.5)
    allowed = (request[:, None] == request[None, :]) & (offset[None, :] <= offset[:, None])
    scores = jnp.where(allowed[None], scores, NEG)
    top_score = jnp.max(scores, axis=2)
    weights = jnp.exp(scores - top_score[:, :, None])
    weight_sum = jnp.sum(weights, axis=2)
    mixed_out = jnp.einsum(
        "hts,she->the", weights.astype(jnp.bfloat16), values, preferred_element_type=jnp.float32
    )
    return (mixed_out, top_score.T, weight_sum.T)


def body(
    tokens_in,
    req_lengths,
    req_groups,
    prefix_cache,
    attn_gain,
    mlp_gain,
    w_qkv,
    w_out,
    w_gate_up,
    w_down,
):
    row_count = tokens_in.shape[0]
    shard_width = tokens_in.shape[1]
    device_row = lax.axis_index("req")
    mp_index = lax.axis_index("mp")
    full_rows = lax.all_gather(tokens_in, "mp", axis=1, tiled=True)
    model_width = full_rows.shape[1]
    normed_attn = layer_norm(full_rows, attn_gain)
    heads = w_qkv.shape[2] // HEAD_DIM
    projected = jnp.dot(
        normed_attn, w_qkv.reshape(model_width, -1), preferred_element_type=jnp.float32
    )
    projected = projected.reshape(row_count, 3, heads, HEAD_DIM)
    length_row = lax.dynamic_index_in_dim(req_lengths, device_row, 0, keepdims=False)
    group_row = lax.dynamic_index_in_dim(req_groups, device_row, 0, keepdims=False)
    request, offset, groups_of = token_meta(length_row, group_row, row_count)
    positions = (PREFIX + offset).astype(jnp.float32)
    query_rot = rotary(projected[:, 0], positions).astype(jnp.bfloat16)
    key_rot = rotary(projected[:, 1], positions).astype(jnp.bfloat16)
    value_rows = projected[:, 2].astype(jnp.bfloat16)
    own_state = own_attention(query_rot, key_rot, value_rows, request, offset)
    group_ids = jnp.arange(GROUPS, dtype=jnp.int32)
    block_rows = prefix_cache.shape[1]
    member = groups_of[:, None] == group_ids[None, :]
    piece = lax.all_gather(prefix_cache, "req", axis=1, tiled=True)

    def step_block(index, carry):
        part = lax.dynamic_slice_in_dim(piece, index * block_rows, block_rows, 1)
        normed_part, part_top, part_sum = rounded_block(query_rot, member, part)
        return combine_states(
            carry, (normed_part.astype(jnp.float32) * part_sum[..., None], part_top, part_sum)
        )

    mixed_out, top_score, weight_sum = lax.fori_loop(
        0, piece.shape[1] // block_rows, step_block, own_state
    )
    attn_rows = (
        (mixed_out / weight_sum[..., None])
        .astype(jnp.bfloat16)
        .reshape(row_count, heads * HEAD_DIM)
    )
    attn_part = jnp.dot(attn_rows, w_out, preferred_element_type=jnp.float32)
    attn_share = lax.psum_scatter(
        attn_part.astype(jnp.bfloat16), "mp", scatter_dimension=1, tiled=True
    ).astype(jnp.float32)
    residual_share = (tokens_in.astype(jnp.float32) + attn_share).astype(jnp.bfloat16)
    residual_f = residual_share.astype(jnp.float32)
    row_sums, row_squares = lax.psum(
        (jnp.sum(residual_f, axis=1), jnp.sum(residual_f * residual_f, axis=1)), "mp"
    )
    row_mean = row_sums / model_width
    variance = row_squares / model_width - row_mean * row_mean
    gain_share = lax.dynamic_slice_in_dim(mlp_gain, mp_index * shard_width, shard_width, 0).astype(
        jnp.float32
    )
    normed_share = (
        (residual_f - row_mean[:, None]) * lax.rsqrt(variance + EPS)[:, None] * gain_share[None, :]
    ).astype(jnp.bfloat16)
    normed_mlp = lax.all_gather(normed_share, "mp", axis=1, tiled=True)
    local_units = w_gate_up.shape[2]
    gate_up = jnp.dot(
        normed_mlp, w_gate_up.reshape(model_width, -1), preferred_element_type=jnp.float32
    ).reshape(row_count, 2, local_units)
    hidden = (jax.nn.silu(gate_up[:, 0]) * gate_up[:, 1]).astype(jnp.bfloat16)
    down_part = jnp.dot(hidden, w_down, preferred_element_type=jnp.float32)
    mlp_share = lax.psum_scatter(
        down_part.astype(jnp.bfloat16), "mp", scatter_dimension=1, tiled=True
    ).astype(jnp.float32)
    return (residual_share.astype(jnp.float32) + mlp_share).astype(jnp.bfloat16)


def solution(mesh):
    return jax.shard_map(
        body,
        mesh=mesh,
        in_specs=(
            P("req", "mp"),
            P(),
            P(),
            P(None, "req", None, "mp"),
            P(),
            P(),
            P(None, None, "mp"),
            P("mp", None),
            P(None, None, "mp"),
            P("mp", None),
        ),
        out_specs=P("req", "mp"),
        check_vma=False,
    )
```

profile of v0, /device:TPU:2, one launch (start us, length us, event | category | flops | bytes accessed | tf_op | source)
XLA Modules:
  0.0 390.6 jit_solution(3455351838395979648)
XLA Ops:
  6.5 2.0 copy.31
  8.6 2.6 copy.29
  11.2 24.8 %all_gather.9 = bf16[128,2048]{1,0:T(8,128)(2,1)S(1)} all-gather(bf16[128,128]{1,0:T(8,128)(2,1)S(1)} %copy-done.3), channel_id=1, replica_groups=mesh['req'=16,'mp'=16] {'mp'}, dimensions={1}, use_global_device_ids=true | all-gather | bytes 557056 | tf_op jit(solution)/shard_map/all_gather | solution.py:119
  39.7 21.0 %all-gather.2.cloned.1.call-done = bf16[2,4096,2,128]{1,3,0,2:T(8,128)(2,1)} async-done(((bf16[2,256,2,128]{1,3,0,2:T(8,128)(2,1)}), bf16[2,4096,2,128]{1,3,0,2:T(8,128)(2,1)}) %all-gather.2.cloned.1.call-update) | async-done | bytes 4194320 | tf_op jit(solution)/shard_map/all_gather | solution.py:138
  60.7 98.9 %while.18 = (s32[]{:T(128)}, f32[128,2,64]{0,2,1:T(8,128)}, f32[128,2]{0,1:T(2,128)S(1)}, f32[128,2]{0,1:T(2,128)S(1)}, bf16[2,4096,2,128]{1,3,0,2:T(8,128)(2,1)...) while((s32[]{:T(128)}, f32[128,2,64]{0,2,1:T(8,128)}, ...), condition=%wide.region_11.12_spmd.clone, body=%wide.region_8.11_spmd.clone.sunk | while | flops 34587912 | bytes 4112575 | solution.py:147
  60.7 1.6 constant_dynamic-slice_fusion.4
  64.9 2.0 fusion.64
  66.9 1.6 constant_dynamic-slice_fusion.4
  71.0 2.0 fusion.64
  73.0 1.6 constant_dynamic-slice_fusion.4
  77.2 2.0 fusion.64
  79.2 1.6 constant_dynamic-slice_fusion.4
  81.1 1.2 fusion.63
  83.4 2.0 fusion.64
  85.4 1.6 constant_dynamic-slice_fusion.4
  89.6 2.0 fusion.64
  91.6 1.6 constant_dynamic-slice_fusion.4
  93.5 1.2 fusion.63
  95.8 2.0 fusion.64
  97.8 1.6 constant_dynamic-slice_fusion.4
  99.6 1.2 fusion.63
  102.0 2.0 fusion.64
  103.9 1.6 constant_dynamic-slice_fusion.4
  108.1 2.0 fusion.64
  110.1 1.6 constant_dynamic-slice_fusion.4
  112.0 1.2 fusion.63
  114.3 2.0 fusion.64
  116.3 1.6 constant_dynamic-slice_fusion.4
  118.2 1.2 fusion.63
  120.5 2.0 fusion.64
  122.5 1.6 constant_dynamic-slice_fusion.4
  126.7 2.0 fusion.64
  128.7 1.6 constant_dynamic-slice_fusion.4
  130.5 1.2 fusion.63
  132.9 2.0 fusion.64
  134.8 1.6 constant_dynamic-slice_fusion.4
  139.0 2.0 fusion.64
  141.0 1.6 constant_dynamic-slice_fusion.4
  145.2 2.0 fusion.64
  147.2 1.6 constant_dynamic-slice_fusion.4
  151.4 2.0 fusion.64
  153.4 1.6 constant_dynamic-slice_fusion.4
  157.6 2.0 fusion.64
  160.4 1.4 convolution_convert_fusion.1
  163.6 76.5 %reduce-scatter.7.cloned.1.call-done = bf16[128,128]{1,0:T(8,128)(2,1)} async-done(((bf16[2048,128]{1,0:T(8,128)(2,1)}), bf16[128,128]{1,0:T(8,128)(2,1)}) %reduce-scatter.7.cloned.1.call-update) | async-done | bytes 32784
  241.1 33.3 %all-reduce = (f32[128]{0:T(128)S(1)}, f32[128]{0:T(128)S(1)}) all-reduce(f32[128]{0:T(128)S(1)} %get-tuple-element.150, f32[128]{0:T(128)S(1)} %get-tuple-element.149), channel_id=1, replica_groups=mesh['req'=16,'mp'=16] {'mp'}, use_global_device_ids=true, to_apply=%region_16.17 | all-reduce | flops 256 | bytes 2048 | tf_op jit(solution)/shard_map/psum | solution.py:161
  274.5 27.3 %all_gather.11 = bf16[128,2048]{1,0:T(8,128)(2,1)S(1)} all-gather(bf16[128,128]{1,0:T(8,128)(2,1)S(1)} %fusion.37), channel_id=1, replica_groups=mesh['req'=16,'mp'=16] {'mp'}, dimensions={1}, use_global_device_ids=true | all-gather | bytes 557056 | tf_op jit(solution)/shard_map/all_gather | solution.py:172
  304.8 77.8 %reduce-scatter.9.cloned.1.call-done = bf16[128,128]{1,0:T(8,128)(2,1)} async-done(((bf16[2048,128]{1,0:T(8,128)(2,1)}), bf16[128,128]{1,0:T(8,128)(2,1)}) %reduce-scatter.9.cloned.1.call-update) | async-done | bytes 32784
  (164 shorter events, 45.3 us)
Async XLA Ops:
  6.5 295.3 %copy-start = (bf16[2048,2,352]{0,2,1:T(8,128)(2,1)S(1)}, bf16[2048,2,352]{0,2,1:T(8,128)(2,1)}, u32[]{:S(2)}) copy-start(bf16[2048,2,352]{0,2,1:T(8,128)(2,1)} %param.20) | copy-start | bytes 8650756
  6.5 54.1 %all-gather.2.cloned.1.call-start = ((), (), s32[]{:S(2)}) async-start(), calls=%async_computation.2 | async-start | bytes 4456448 | tf_op jit(solution)/shard_map/all_gather | solution.py:138
  8.5 231.6 %reduce-scatter.7.cloned.1.call-start = ((), (), s32[]{:S(2)}) async-start(), calls=%async_computation.3 | async-start | bytes 557056
  8.6 2.6 copy-start.5
  8.6 2.6 copy-start.3
  11.2 25.2 %copy-start.1 = (bf16[2048,3,128]{0,2,1:T(8,128)(2,1)S(1)}, bf16[2048,3,128]{0,2,1:T(8,128)(2,1)}, u32[]{:S(2)}) copy-start(bf16[2048,3,128]{0,2,1:T(8,128)(2,1)} %copy.29) | copy-start | bytes 4718596
  36.5 0.7 copy-start.6
  36.5 0.7 copy-start.7
  159.6 81.4 %copy-start.4 = (bf16[128,128]{1,0:T(8,128)(2,1)S(1)}, bf16[128,128]{1,0:T(8,128)(2,1)}, u32[]{:S(2)}) copy-start(bf16[128,128]{1,0:T(8,128)(2,1)} %param.12) | copy-start | bytes 98308
  162.8 219.8 %reduce-scatter.9.cloned.1.call-start = ((), (), s32[]{:S(2)}) async-start(), calls=%async_computation.4 | async-start | bytes 557056
  301.9 1.4 copy-start.2
Sparse Core Ops, SparseCore 0:
  9.1 51.5 all-gather.1
  162.9 77.1 reduce-scatter.6
  304.9 77.6 reduce-scatter.8
where the time goes:
time: 392 us; the launch traced here: 391 us
  waiting for transfers between devices  175 us (45%)
  blocking collectives  85.4 us (22%)
  matrix products  55.5 us (14%)
  local copies, waits for them, and re-layouts  54.7 us (14%)
  between operations  13.3 us (3%)
  other arithmetic  6.08 us (2%)
    unnamed x5, waiting for transfers between devices  154 us
    psum x1, blocking collectives, body(): lax.psum((jnp.sum(residual_f, axis=1), jnp.sum(residual_f * residual_f, a...  33.3 us
    dot_general x16, matrix products, rounded_block(): jnp.einsum('hts,she->the', weights.astype(jnp.bfloat16), value_part, pref...  31.8 us
    all_gather x1, blocking collectives, body(): normed_mlp = lax.all_gather(normed_share, 'mp', axis=1, tiled=True)  27.3 us
    slice x16, local copies, waits for them, and re-layouts, rounded_block(): key_part = part[:, :, 0].reshape(group_count, block, heads, HEAD_DIM)  26.1 us
    all_gather x1, blocking collectives, body(): full_rows = lax.all_gather(tokens_in, 'mp', axis=1, tiled=True)  24.8 us
    all_gather x1, waiting for transfers between devices, body(): piece = lax.all_gather(prefix_cache, 'req', axis=1, tiled=True)  21 us
    dot_general x16, matrix products, rounded_block(): jnp.einsum('thd,gnhd->htgn', query, key_part, preferred_element_type=jnp....  19.2 us
  transfers between devices with their start and end apart: 3, of which 3 were waited for; matrix products, arithmetic and copies ran while one was open for 2% of the time, Pallas kernels for 0%

commit v1 on v0

--- a/solution.py
+++ b/solution.py
@@ -9,6 +9,27 @@
 GROUPS = 2
 NEG = -1e30
 EPS = 1e-05
+
+
+def gather_around(x, axis, dim):
+    count, index, extent = (lax.axis_size(axis), lax.axis_index(axis), x.shape[dim])
+    right = [(i, (i + 1) % count) for i in range(count)]
+    backward = [(i, (i - 1) % count) for i in range(count)]
+    out = jnp.zeros((*x.shape[:dim], count * extent, *x.shape[dim + 1 :]), x.dtype)
+    out = lax.dynamic_update_slice_in_dim(out, x, index * extent, axis=dim)
+    from_left = from_right = x
+    halfway = count // 2
+    for step in range(1, halfway + 1):
+        from_left = lax.ppermute(from_left, axis, right)
+        out = lax.dynamic_update_slice_in_dim(
+            out, from_left, (index - step) % count * extent, axis=dim
+        )
+        if step < count - halfway:
+            from_right = lax.ppermute(from_right, axis, backward)
+            out = lax.dynamic_update_slice_in_dim(
+                out, from_right, (index + step) % count * extent, axis=dim
+            )
+    return out
 
 
 def layer_norm(rows_in, gain_vec):
@@ -116,7 +137,7 @@
     shard_width = tokens_in.shape[1]
     device_row = lax.axis_index("req")
     mp_index = lax.axis_index("mp")
-    full_rows = lax.all_gather(tokens_in, "mp", axis=1, tiled=True)
+    full_rows = gather_around(tokens_in, "mp", 1)
     model_width = full_rows.shape[1]
     normed_attn = layer_norm(full_rows, attn_gain)
     heads = w_qkv.shape[2] // HEAD_DIM

time: 392 us -> 404 us (1.031)
  starting transfers between devices: 0.09 us -> 29.2 us
  blocking collectives: 85.4 us -> 60.6 us
  waiting for transfers between devices: 175 us -> 180 us
    ppermute x0 -> x15, starting transfers between devices: none -> 29.1 us  [the longest x7 27.3 us: gather_around(): from_right = lax.ppermute(from_right, axis, backward)]
    all_gather x1 -> x0, blocking collectives: 24.8 us -> none  [body(): full_rows = lax.all_gather(tokens_in, 'mp', axis=1, tiled=True)]
    all_gather x1, waiting for transfers between devices: 21 us -> 0.01 us  [body(): piece = lax.all_gather(prefix_cache, 'req', axis=1, tiled=True)]
    ppermute x0 -> x15, waiting for transfers between devices: none -> 17.2 us  [the longest x8 17.2 us: gather_around(): from_left = lax.ppermute(from_left, axis, right)]
    unnamed x5, waiting for transfers between devices: 154 us -> 163 us
    unnamed x22 -> x16, local copies, waits for them, and re-layouts: 8.77 us -> 8.75 us
  transfers between devices with their start and end apart: 3 -> 18, of which waited for: 3 -> 9; matrix products, arithmetic and copies ran while one was open for 2% -> 2% of each run, Pallas kernels for 0% -> 0%
where the time goes in v1:
time: 404 us; the launch traced here: 403 us
  waiting for transfers between devices  180 us (45%)
  blocking collectives  60.6 us (15%)
  local copies, waits for them, and re-layouts  56.3 us (14%)
  matrix products  55.5 us (14%)
  starting transfers between devices  29.2 us (7%)
  between operations  13.4 us (3%)
  other arithmetic  6.89 us (2%)
    unnamed x5, waiting for transfers between devices  163 us
    psum x1, blocking collectives, body(): lax.psum((jnp.sum(residual_f, axis=1), jnp.sum(residual_f * residual_f, a...  33.3 us
    dot_general x16, matrix products, rounded_block(): jnp.einsum('hts,she->the', weights.astype(jnp.bfloat16), value_part, pref...  31.8 us
    ppermute x7, starting transfers between devices, gather_around(): from_right = lax.ppermute(from_right, axis, backward)  27.3 us
    all_gather x1, blocking collectives, body(): normed_mlp = lax.all_gather(normed_share, 'mp', axis=1, tiled=True)  27.3 us
    slice x16, local copies, waits for them, and re-layouts, rounded_block(): key_part = part[:, :, 0].reshape(group_count, block, heads, HEAD_DIM)  26.1 us
    dot_general x16, matrix products, rounded_block(): jnp.einsum('thd,gnhd->htgn', query, key_part, preferred_element_type=jnp....  19.2 us
    ppermute x8, waiting for transfers between devices, gather_around(): from_left = lax.ppermute(from_left, axis, right)  17.2 us
  transfers between devices with their start and end apart: 18, of which 9 were waited for; matrix products, arithmetic and copies ran while one was open for 2% of the time, Pallas kernels for 0%

profile of v1, /device:TPU:2, one launch (start us, length us, event | category | flops | bytes accessed | tf_op | source)
XLA Modules:
  0.0 402.5 jit_solution(10997921958284131445)
XLA Ops:
  6.5 2.0 copy.31
  8.6 1.7 collective-permute-start
  10.2 2.6 collective-permute-start.1
  15.8 2.6 copy.29
  18.5 4.1 %collective-permute-start.3 = (bf16[128,128]{1,0:T(8,128)(2,1)S(1)}, bf16[128,128]{1,0:T(8,128)(2,1)S(1)}, u32[]{:S(2)}, u32[]{:S(2)}) collective-permute-start(bf16[128,128]{1,0:T(8,128)(2,1)S(1)} %collective-permute-done.1), channel_id=1, source_target_pairs={{0,15},{1,0},{2,1},{3,2},{4,3},{5,4},{6,5},{7,6},{8,7},{9,8},{10,9... | collective-permute-start | bytes 98312 | tf_op jit(solution)/shard_map/ppermute | solution.py:28
  22.7 1.8 collective-permute-done.2
  24.5 4.1 %collective-permute-start.5 = (bf16[128,128]{1,0:T(8,128)(2,1)S(1)}, bf16[128,128]{1,0:T(8,128)(2,1)S(1)}, u32[]{:S(2)}, u32[]{:S(2)}) collective-permute-start(bf16[128,128]{1,0:T(8,128)(2,1)S(1)} %collective-permute-done.3), channel_id=1, source_target_pairs={{0,15},{1,0},{2,1},{3,2},{4,3},{5,4},{6,5},{7,6},{8,7},{9,8},{10,9... | collective-permute-start | bytes 98312 | tf_op jit(solution)/shard_map/ppermute | solution.py:28
  28.7 1.8 collective-permute-done.4
  30.6 4.1 %collective-permute-start.7 = (bf16[128,128]{1,0:T(8,128)(2,1)S(1)}, bf16[128,128]{1,0:T(8,128)(2,1)S(1)}, u32[]{:S(2)}, u32[]{:S(2)}) collective-permute-start(bf16[128,128]{1,0:T(8,128)(2,1)S(1)} %collective-permute-done.5), channel_id=1, source_target_pairs={{0,15},{1,0},{2,1},{3,2},{4,3},{5,4},{6,5},{7,6},{8,7},{9,8},{10,9... | collective-permute-start | bytes 98312 | tf_op jit(solution)/shard_map/ppermute | solution.py:28
  34.7 1.8 collective-permute-done.6
  36.6 4.1 %collective-permute-start.9 = (bf16[128,128]{1,0:T(8,128)(2,1)S(1)}, bf16[128,128]{1,0:T(8,128)(2,1)S(1)}, u32[]{:S(2)}, u32[]{:S(2)}) collective-permute-start(bf16[128,128]{1,0:T(8,128)(2,1)S(1)} %collective-permute-done.7), channel_id=1, source_target_pairs={{0,15},{1,0},{2,1},{3,2},{4,3},{5,4},{6,5},{7,6},{8,7},{9,8},{10,9... | collective-permute-start | bytes 98312 | tf_op jit(solution)/shard_map/ppermute | solution.py:28
  40.8 1.9 collective-permute-done.8
  42.7 4.1 %collective-permute-start.11 = (bf16[128,128]{1,0:T(8,128)(2,1)S(1)}, bf16[128,128]{1,0:T(8,128)(2,1)S(1)}, u32[]{:S(2)}, u32[]{:S(2)}) collective-permute-start(bf16[128,128]{1,0:T(8,128)(2,1)S(1)} %collective-permute-done.9), channel_id=1, source_target_pairs={{0,15},{1,0},{2,1},{3,2},{4,3},{5,4},{6,5},{7,6},{8,7},{9,8},{10,9... | collective-permute-start | bytes 98312 | tf_op jit(solution)/shard_map/ppermute | solution.py:28
  46.9 1.8 collective-permute-done.10
  48.7 4.1 %collective-permute-start.13 = (bf16[128,128]{1,0:T(8,128)(2,1)S(1)}, bf16[128,128]{1,0:T(8,128)(2,1)S(1)}, u32[]{:S(2)}, u32[]{:S(2)}) collective-permute-start(bf16[128,128]{1,0:T(8,128)(2,1)S(1)} %collective-permute-done.11), channel_id=1, source_target_pairs={{0,15},{1,0},{2,1},{3,2},{4,3},{5,4},{6,5},{7,6},{8,7},{9,8},{10,9... | collective-permute-start | bytes 98312 | tf_op jit(solution)/shard_map/ppermute | solution.py:28
  52.9 1.8 collective-permute-done.12
  54.8 6.0 %collective-permute-done.14 = bf16[128,128]{1,0:T(8,128)(2,1)S(1)} collective-permute-done((bf16[128,128]{1,0:T(8,128)(2,1)S(1)}, bf16[128,128]{1,0:T(8,128)(2,1)S(1)}, u32[]{:S(2)}, u32[]{:S(2)}) %collective-permute-start.14) | collective-permute-done | bytes 32800 | tf_op jit(solution)/shard_map/ppermute | solution.py:23
  63.7 98.9 %while.18 = (s32[]{:T(128)}, f32[128,2,64]{0,2,1:T(8,128)}, f32[128,2]{0,1:T(2,128)S(1)}, f32[128,2]{0,1:T(2,128)S(1)}, bf16[2,4096,2,128]{1,3,0,2:T(8,128)(2,1)...) while((s32[]{:T(128)}, f32[128,2,64]{0,2,1:T(8,128)}, ...), condition=%wide.region_11.12_spmd.clone, body=%wide.region_8.11_spmd.clone.sunk | while | flops 34587912 | bytes 4112575 | solution.py:168
  63.7 1.6 constant_dynamic-slice_fusion.5
  67.8 2.0 fusion.65
  69.8 1.6 constant_dynamic-slice_fusion.5
  74.0 2.0 fusion.65
  76.0 1.6 constant_dynamic-slice_fusion.5
  80.2 2.0 fusion.65
  82.2 1.6 constant_dynamic-slice_fusion.5
  86.4 2.0 fusion.65
  88.4 1.6 constant_dynamic-slice_fusion.5
  92.6 2.0 fusion.65
  94.6 1.6 constant_dynamic-slice_fusion.5
  98.8 2.0 fusion.65
  100.7 1.6 constant_dynamic-slice_fusion.5
  104.9 2.0 fusion.65
  111.1 2.0 fusion.65
  117.3 2.0 fusion.65
  119.3 1.6 constant_dynamic-slice_fusion.5
  123.5 2.0 fusion.65
  129.7 2.0 fusion.65
  131.6 1.6 constant_dynamic-slice_fusion.5
  135.8 2.0 fusion.65
  142.0 2.0 fusion.65
  148.2 2.0 fusion.65
  150.2 1.6 constant_dynamic-slice_fusion.5
  154.4 2.0 fusion.65
  160.6 2.0 fusion.65
  166.6 85.4 %reduce-scatter.7.cloned.1.call-done = bf16[128,128]{1,0:T(8,128)(2,1)} async-done(((bf16[2048,128]{1,0:T(8,128)(2,1)}), bf16[128,128]{1,0:T(8,128)(2,1)}) %reduce-scatter.7.cloned.1.call-update) | async-done | bytes 32784
  253.0 33.3 %all-reduce = (f32[128]{0:T(128)S(1)}, f32[128]{0:T(128)S(1)}) all-reduce(f32[128]{0:T(128)S(1)} %get-tuple-element.150, f32[128]{0:T(128)S(1)} %get-tuple-element.149), channel_id=1, replica_groups=mesh['req'=16,'mp'=16] {'mp'}, use_global_device_ids=true, to_apply=%region_16.17 | all-reduce | flops 256 | bytes 2048 | tf_op jit(solution)/shard_map/psum | solution.py:182
  286.5 27.3 %all_gather.7 = bf16[128,2048]{1,0:T(8,128)(2,1)S(1)} all-gather(bf16[128,128]{1,0:T(8,128)(2,1)S(1)} %fusion.37), channel_id=1, replica_groups=mesh['req'=16,'mp'=16] {'mp'}, dimensions={1}, use_global_device_ids=true | all-gather | bytes 557056 | tf_op jit(solution)/shard_map/all_gather | solution.py:193
  316.6 77.9 %reduce-scatter.9.cloned.1.call-done = bf16[128,128]{1,0:T(8,128)(2,1)} async-done(((bf16[2048,128]{1,0:T(8,128)(2,1)}), bf16[128,128]{1,0:T(8,128)(2,1)}) %reduce-scatter.9.cloned.1.call-update) | async-done | bytes 32784
  (204 shorter events, 66.2 us)
Async XLA Ops:
  6.5 307.2 %copy-start = (bf16[2048,2,352]{0,2,1:T(8,128)(2,1)S(1)}, bf16[2048,2,352]{0,2,1:T(8,128)(2,1)}, u32[]{:S(2)}) copy-start(bf16[2048,2,352]{0,2,1:T(8,128)(2,1)} %param.20) | copy-start | bytes 8650756
  6.5 57.1 %all-gather.2.cloned.1.call-start = ((), (), s32[]{:S(2)}) async-start(), calls=%async_computation.2 | async-start | bytes 4456448 | tf_op jit(solution)/shard_map/all_gather | solution.py:159
  8.5 243.5 %reduce-scatter.7.cloned.1.call-start = ((), (), s32[]{:S(2)}) async-start(), calls=%async_computation.3 | async-start | bytes 557056
  8.6 9.8 %collective-permute-start = (bf16[128,128]{1,0:T(8,128)(2,1)}, bf16[128,128]{1,0:T(8,128)(2,1)S(1)}, u32[]{:S(2)}, u32[]{:S(2)}) collective-permute-start(bf16[128,128]{1,0:T(8,128)(2,1)} %param.12), channel_id=1, source_target_pairs={{0,1},{1,2},{2,3},{3,4},{4,5},{5,6},{6,7},{7,8},{8,9},{9,10},{10,1... | collective-permute-start | bytes 98312 | tf_op jit(solution)/shard_map/ppermute | solution.py:23
  10.2 8.3 %collective-permute-start.1 = (bf16[128,128]{1,0:T(8,128)(2,1)}, bf16[128,128]{1,0:T(8,128)(2,1)S(1)}, u32[]{:S(2)}, u32[]{:S(2)}) collective-permute-start(bf16[128,128]{1,0:T(8,128)(2,1)} %param.12), channel_id=1, source_target_pairs={{0,15},{1,0},{2,1},{3,2},{4,3},{5,4},{6,5},{7,6},{8,7},{9,8},{10,9... | collective-permute-start | bytes 98312 | tf_op jit(solution)/shard_map/ppermute | solution.py:28
  15.8 2.6 copy-start.4
  18.4 42.8 %copy-start.1 = (bf16[2048,3,128]{0,2,1:T(8,128)(2,1)S(1)}, bf16[2048,3,128]{0,2,1:T(8,128)(2,1)}, u32[]{:S(2)}) copy-start(bf16[2048,3,128]{0,2,1:T(8,128)(2,1)} %copy.29) | copy-start | bytes 4718596
  18.4 6.1 %collective-permute-start.2 = (bf16[128,128]{1,0:T(8,128)(2,1)S(1)}, bf16[128,128]{1,0:T(8,128)(2,1)S(1)}, u32[]{:S(2)}, u32[]{:S(2)}) collective-permute-start(bf16[128,128]{1,0:T(8,128)(2,1)S(1)} %collective-permute-done), channel_id=1, source_target_pairs={{0,1},{1,2},{2,3},{3,4},{4,5},{5,6},{6,7},{7,8},{8,9},{9,10},{10,1... | collective-permute-start | bytes 98312 | tf_op jit(solution)/shard_map/ppermute | solution.py:23
  18.5 6.0 %collective-permute-start.3 = (bf16[128,128]{1,0:T(8,128)(2,1)S(1)}, bf16[128,128]{1,0:T(8,128)(2,1)S(1)}, u32[]{:S(2)}, u32[]{:S(2)}) collective-permute-start(bf16[128,128]{1,0:T(8,128)(2,1)S(1)} %collective-permute-done.1), channel_id=1, source_target_pairs={{0,15},{1,0},{2,1},{3,2},{4,3},{5,4},{6,5},{7,6},{8,7},{9,8},{10,9... | collective-permute-start | bytes 98312 | tf_op jit(solution)/shard_map/ppermute | solution.py:28
  24.5 6.0 %collective-permute-start.4 = (bf16[128,128]{1,0:T(8,128)(2,1)S(1)}, bf16[128,128]{1,0:T(8,128)(2,1)S(1)}, u32[]{:S(2)}, u32[]{:S(2)}) collective-permute-start(bf16[128,128]{1,0:T(8,128)(2,1)S(1)} %collective-permute-done.2), channel_id=1, source_target_pairs={{0,1},{1,2},{2,3},{3,4},{4,5},{5,6},{6,7},{7,8},{8,9},{9,10},{10,1... | collective-permute-start | bytes 98312 | tf_op jit(solution)/shard_map/ppermute | solution.py:23
  24.5 6.0 %collective-permute-start.5 = (bf16[128,128]{1,0:T(8,128)(2,1)S(1)}, bf16[128,128]{1,0:T(8,128)(2,1)S(1)}, u32[]{:S(2)}, u32[]{:S(2)}) collective-permute-start(bf16[128,128]{1,0:T(8,128)(2,1)S(1)} %collective-permute-done.3), channel_id=1, source_target_pairs={{0,15},{1,0},{2,1},{3,2},{4,3},{5,4},{6,5},{7,6},{8,7},{9,8},{10,9... | collective-permute-start | bytes 98312 | tf_op jit(solution)/shard_map/ppermute | solution.py:28
  30.6 6.0 %collective-permute-start.6 = (bf16[128,128]{1,0:T(8,128)(2,1)S(1)}, bf16[128,128]{1,0:T(8,128)(2,1)S(1)}, u32[]{:S(2)}, u32[]{:S(2)}) collective-permute-start(bf16[128,128]{1,0:T(8,128)(2,1)S(1)} %collective-permute-done.4), channel_id=1, source_target_pairs={{0,1},{1,2},{2,3},{3,4},{4,5},{5,6},{6,7},{7,8},{8,9},{9,10},{10,1... | collective-permute-start | bytes 98312 | tf_op jit(solution)/shard_map/ppermute | solution.py:23
  30.6 6.0 %collective-permute-start.7 = (bf16[128,128]{1,0:T(8,128)(2,1)S(1)}, bf16[128,128]{1,0:T(8,128)(2,1)S(1)}, u32[]{:S(2)}, u32[]{:S(2)}) collective-permute-start(bf16[128,128]{1,0:T(8,128)(2,1)S(1)} %collective-permute-done.5), channel_id=1, source_target_pairs={{0,15},{1,0},{2,1},{3,2},{4,3},{5,4},{6,5},{7,6},{8,7},{9,8},{10,9... | collective-permute-start | bytes 98312 | tf_op jit(solution)/shard_map/ppermute | solution.py:28
  36.6 6.1 %collective-permute-start.8 = (bf16[128,128]{1,0:T(8,128)(2,1)S(1)}, bf16[128,128]{1,0:T(8,128)(2,1)S(1)}, u32[]{:S(2)}, u32[]{:S(2)}) collective-permute-start(bf16[128,128]{1,0:T(8,128)(2,1)S(1)} %collective-permute-done.6), channel_id=1, source_target_pairs={{0,1},{1,2},{2,3},{3,4},{4,5},{5,6},{6,7},{7,8},{8,9},{9,10},{10,1... | collective-permute-start | bytes 98312 | tf_op jit(solution)/shard_map/ppermute | solution.py:23
  36.6 6.1 %collective-permute-start.9 = (bf16[128,128]{1,0:T(8,128)(2,1)S(1)}, bf16[128,128]{1,0:T(8,128)(2,1)S(1)}, u32[]{:S(2)}, u32[]{:S(2)}) collective-permute-start(bf16[128,128]{1,0:T(8,128)(2,1)S(1)} %collective-permute-done.7), channel_id=1, source_target_pairs={{0,15},{1,0},{2,1},{3,2},{4,3},{5,4},{6,5},{7,6},{8,7},{9,8},{10,9... | collective-permute-start | bytes 98312 | tf_op jit(solution)/shard_map/ppermute | solution.py:28
  42.7 6.0 %collective-permute-start.10 = (bf16[128,128]{1,0:T(8,128)(2,1)S(1)}, bf16[128,128]{1,0:T(8,128)(2,1)S(1)}, u32[]{:S(2)}, u32[]{:S(2)}) collective-permute-start(bf16[128,128]{1,0:T(8,128)(2,1)S(1)} %collective-permute-done.8), channel_id=1, source_target_pairs={{0,1},{1,2},{2,3},{3,4},{4,5},{5,6},{6,7},{7,8},{8,9},{9,10},{10,1... | collective-permute-start | bytes 98312 | tf_op jit(solution)/shard_map/ppermute | solution.py:23
  42.7 6.0 %collective-permute-start.11 = (bf16[128,128]{1,0:T(8,128)(2,1)S(1)}, bf16[128,128]{1,0:T(8,128)(2,1)S(1)}, u32[]{:S(2)}, u32[]{:S(2)}) collective-permute-start(bf16[128,128]{1,0:T(8,128)(2,1)S(1)} %collective-permute-done.9), channel_id=1, source_target_pairs={{0,15},{1,0},{2,1},{3,2},{4,3},{5,4},{6,5},{7,6},{8,7},{9,8},{10,9... | collective-permute-start | bytes 98312 | tf_op jit(solution)/shard_map/ppermute | solution.py:28
  48.7 6.0 %collective-permute-start.12 = (bf16[128,128]{1,0:T(8,128)(2,1)S(1)}, bf16[128,128]{1,0:T(8,128)(2,1)S(1)}, u32[]{:S(2)}, u32[]{:S(2)}) collective-permute-start(bf16[128,128]{1,0:T(8,128)(2,1)S(1)} %collective-permute-done.10), channel_id=1, source_target_pairs={{0,1},{1,2},{2,3},{3,4},{4,5},{5,6},{6,7},{7,8},{8,9},{9,10},{10,1... | collective-permute-start | bytes 98312 | tf_op jit(solution)/shard_map/ppermute | solution.py:23
  48.7 6.0 %collective-permute-start.13 = (bf16[128,128]{1,0:T(8,128)(2,1)S(1)}, bf16[128,128]{1,0:T(8,128)(2,1)S(1)}, u32[]{:S(2)}, u32[]{:S(2)}) collective-permute-start(bf16[128,128]{1,0:T(8,128)(2,1)S(1)} %collective-permute-done.11), channel_id=1, source_target_pairs={{0,15},{1,0},{2,1},{3,2},{4,3},{5,4},{6,5},{7,6},{8,7},{9,8},{10,9... | collective-permute-start | bytes 98312 | tf_op jit(solution)/shard_map/ppermute | solution.py:28
  54.7 6.0 %collective-permute-start.14 = (bf16[128,128]{1,0:T(8,128)(2,1)S(1)}, bf16[128,128]{1,0:T(8,128)(2,1)S(1)}, u32[]{:S(2)}, u32[]{:S(2)}) collective-permute-start(bf16[128,128]{1,0:T(8,128)(2,1)S(1)} %collective-permute-done.12), channel_id=1, source_target_pairs={{0,1},{1,2},{2,3},{3,4},{4,5},{5,6},{6,7},{7,8},{8,9},{9,10},{10,1... | collective-permute-start | bytes 98312 | tf_op jit(solution)/shard_map/ppermute | solution.py:23
  162.6 90.4 %copy-start.3 = (bf16[128,128]{1,0:T(8,128)(2,1)S(1)}, bf16[128,128]{1,0:T(8,128)(2,1)}, u32[]{:S(2)}) copy-start(bf16[128,128]{1,0:T(8,128)(2,1)} %param.12) | copy-start | bytes 98308
  165.8 228.7 %reduce-scatter.9.cloned.1.call-start = ((), (), s32[]{:S(2)}) async-start(), calls=%async_computation.4 | async-start | bytes 557056
  313.7 1.4 copy-start.2
Sparse Core Ops, SparseCore 0:
  9.1 51.8 all-gather.1
  165.9 86.0 reduce-scatter.6
  316.7 77.6 reduce-scatter.8
